TPU v7x, 32 devices: a whole 2x2x4 slice. The times are simulated.
32 devices in a mesh: slab: 2 (over x), freq: 4 (over y, core), energy: 4 (over z).
Axes of the slice: x: 2, y: 2, z: 4, core: 2. Of those that a mesh axis runs over, the one named last changes fastest.
Arguments:
- lesser: bfloat16 [8, 4, 2, 512, 512], P('energy', 'slab'), may hold values from -6 to 6
- retarded: bfloat16 [8, 4, 2, 512, 512], P('energy', 'slab'), may hold values from -0.25 to 0.25
- coupling: bfloat16 [8, 512, 512], P('freq'), may hold values from -0.125 to 0.125
- occupations: float32 [8], P('freq'), may hold values from 0.1 to 3
- offsets: int32 [8], P('freq'), may hold values from 1 to 2
- intersection: float32 [4], P('slab'), may hold values from 0.2 to 0.6
Outputs:
- updated: float32 [8, 4, 2, 512, 512], P('energy', 'slab', None, 'freq')
All inputs are finite; a program needn't handle non-finite values.
Results may differ from a plain program's by a relative error of at most 0.017.
Values may be sent and summed in bfloat16 or wider, within the bound.
A program may use at most 128 MiB of HBM per device.

v0:
```python
import jax
import jax.numpy as jnp
from jax import lax
from jax.sharding import PartitionSpec as P

NO = 512
OFFMAX = 2


def with_halo(block, sides, width):
    for axis, dim in sides:
        count = lax.axis_size(axis)
        forward = [(i, i + 1) for i in range(count - 1)]
        backward = [(target, source) for source, target in forward]
        low = lax.ppermute(
            lax.slice_in_dim(block, block.shape[dim] - width, None, axis=dim), axis, forward
        )
        high = lax.ppermute(lax.slice_in_dim(block, 0, width, axis=dim), axis, backward)
        block = jnp.concatenate([low, block, high], axis=dim)
    return block


def shards(lesser, retarded, coupling, occupations, offsets, intersection):
    freq_count = lax.axis_size("freq")
    row_count = NO // freq_count
    row_first = lax.axis_index("freq") * row_count
    padded = with_halo(lesser, (("energy", 0),), OFFMAX)
    energy_count = lesser.shape[0]
    positions = jnp.arange(energy_count, dtype=jnp.int32)[None, :] + OFFMAX
    lower_green = jnp.take(padded, positions - offsets[:, None], axis=0)
    upper_green = jnp.take(padded, positions + offsets[:, None], axis=0)
    scale = occupations[:, None, None, None, None, None]
    mixture = (
        scale * lower_green.astype(jnp.float32) + (scale + 1.0) * upper_green.astype(jnp.float32)
    ).astype(jnp.bfloat16)
    real_green = retarded[:, :, 0]
    imag_green = retarded[:, :, 1]
    real_rows = lax.dynamic_slice_in_dim(real_green, row_first, row_count, 2)
    imag_rows = lax.dynamic_slice_in_dim(imag_green, row_first, row_count, 2)
    left_product = jnp.einsum(
        "fri,fescij->fescrj", coupling, mixture, preferred_element_type=jnp.float32
    ).astype(jnp.bfloat16)
    self_energy = lax.psum_scatter(
        jnp.einsum(
            "fescrj,fkj->resck", left_product, coupling, preferred_element_type=jnp.float32
        ).astype(jnp.bfloat16),
        "freq",
        scatter_dimension=0,
        tiled=True,
    )
    beside_all = with_halo(self_energy, (("slab", 2),), 1)
    beside = beside_all[:, :, :-2].astype(jnp.float32) + beside_all[:, :, 2:].astype(jnp.float32)
    total = self_energy.astype(jnp.float32) + intersection[None, None, :, None, None] * beside
    combined = total.astype(jnp.bfloat16)
    real_self = combined[:, :, :, 0]
    imag_self = combined[:, :, :, 1]

    def by_transpose(left_side, right_side):
        return jnp.einsum(
            "resj,eskj->resk", left_side, right_side, preferred_element_type=jnp.float32
        )

    real_part = by_transpose(real_self, real_green) + by_transpose(imag_self, imag_green)
    imag_part = by_transpose(imag_self, real_green) - by_transpose(real_self, imag_green)
    product = jnp.stack([real_part, imag_part], axis=3).astype(jnp.bfloat16)
    y_piece = lax.all_gather(product, "freq", axis=0, tiled=True)
    real_piece = y_piece[:, :, :, 0]
    imag_piece = y_piece[:, :, :, 1]

    def plain_product(left_side, right_side):
        return jnp.einsum(
            "esrm,mesk->esrk", left_side, right_side, preferred_element_type=jnp.float32
        )

    out_real = plain_product(real_rows, real_piece) - plain_product(imag_rows, imag_piece)
    out_imag = plain_product(real_rows, imag_piece) + plain_product(imag_rows, real_piece)
    return jnp.stack([out_real, out_imag], axis=2)


def solution(mesh):
    return jax.shard_map(
        shards,
        mesh=mesh,
        in_specs=(
            P("energy", "slab", None, None, None),
            P("energy", "slab", None, None, None),
            P("freq", None, None),
            P("freq"),
            P("freq"),
            P("slab"),
        ),
        out_specs=P("energy", "slab", None, "freq", None),
        check_vma=False,
    )
```

profile of v0, /device:TPU:0, one launch (start us, length us, event | category | flops | bytes accessed | tf_op | source)
XLA Modules:
  0.0 271.4 jit_solution(2159520108255481888)
XLA Ops:
  6.5 7.0 %collective-permute-start = (bf16[2,2,2,512,512]{4,3,2,1,0:T(8,128)(2,1)}, bf16[2,2,2,512,512]{4,3,2,1,0:T(8,128)(2,1)}, u32[]{:S(2)}, u32[]{:S(2)}) collective-permute-start(bf16[2,2,2,512,512]{4,3,2,1,0:T(8,128)(2,1)} %param.8), channel_id=1, source_target_pairs={{0,1},{1,2},{2,3},{4,5},{5,6},{6,7},{8,9},{9,10},{10,11},{12,13},{... | collective-permute-start | bytes 12582920 | tf_op jit(solution)/shard_map/ppermute | solution.py:15
  13.6 1.3 collective-permute-start.1
  14.9 0.7 compare_select_fusion
  17.2 84.6 %collective-permute-done = bf16[2,2,2,512,512]{4,3,2,1,0:T(8,128)(2,1)} collective-permute-done((bf16[2,2,2,512,512]{4,3,2,1,0:T(8,128)(2,1)}, bf16[2,2,2,512,512]{4,3,2,1,0:T(8,128)(2,1)}, u32[]{:S(2)}, u32[]{:S(2)}) %collective-permute-start) | collective-permute-done | bytes 4194336 | tf_op jit(solution)/shard_map/ppermute | solution.py:15
  101.8 2.6 constant_dynamic-update-slice_fusion.2
  104.4 0.7 constant_dynamic-update-slice_fusion.1
  105.2 2.6 collective-permute-done.1
  107.8 2.7 %constant_dynamic-update-slice_fusion = bf16[6,2,2,512,512]{4,3,2,1,0:T(8,128)(2,1)S(1)} fusion(bf16[6,2,2,512,512]{4,3,2,1,0:T(8,128)(2,1)S(1)} %constant_dynamic-update-slice_fusion.1, bf16[2,2,2,512,512]{4,3,2,1,0:T(8,128)(2,1)} %collective-permute-done.1), kind=kLoop, calls=%fused_computation.60 | loop fusion | bytes 8388608 | tf_op jit(solution)/shard_map/concatenate | solution.py:19
  110.5 5.1 %fusion.66 = (bf16[6,2,2,256,512]{4,3,2,1,0:T(8,128)(2,1)}, bf16[6,2,2,256,512]{4,3,2,1,0:T(8,128)(2,1)}) fusion(bf16[6,2,2,512,512]{4,3,2,1,0:T(8,128)(2,1)S(1)} %constant_dynamic-update-slice_fusion), kind=kLoop, calls=%fused_computation.75 | loop fusion | bytes 25165824 | tf_op jit(solution)/shard_map/jit(_take)/gather | solution.py:30
  115.7 5.5 %gather_fusion.1 = bf16[4,2,2,256,512]{4,3,2,1,0:T(8,128)(2,1)} fusion(bf16[6,2,2,256,512]{4,3,2,1,0:T(8,128)(2,1)} %get-tuple-element.7, s32[1024]{0:T(1024)S(1)} %get-tuple-element.17), kind=kCustom, calls=%fused_computation.1.clone | custom fusion | bytes 8388624 | tf_op jit(solution)/shard_map/jit(_take)/gather | solution.py:30
  121.2 5.5 %gather_fusion = bf16[4,2,2,256,512]{4,3,2,1,0:T(8,128)(2,1)} fusion(bf16[6,2,2,256,512]{4,3,2,1,0:T(8,128)(2,1)} %get-tuple-element.6, s32[1024]{0:T(1024)S(1)} %get-tuple-element.17), kind=kCustom, calls=%fused_computation.clone | custom fusion | bytes 8388624 | tf_op jit(solution)/shard_map/jit(_take)/gather | solution.py:30
  126.7 5.6 %gather_fusion.3 = bf16[4,2,2,256,512]{4,3,2,1,0:T(8,128)(2,1)} fusion(bf16[6,2,2,256,512]{4,3,2,1,0:T(8,128)(2,1)} %get-tuple-element.7, s32[1024]{0:T(1024)S(1)} %get-tuple-element.16), kind=kCustom, calls=%fused_computation.3.clone | custom fusion | bytes 8388624 | tf_op jit(solution)/shard_map/jit(_take)/gather | solution.py:31
  132.3 5.7 %gather_fusion.2 = bf16[4,2,2,256,512]{4,3,2,1,0:T(8,128)(2,1)} fusion(bf16[6,2,2,256,512]{4,3,2,1,0:T(8,128)(2,1)} %get-tuple-element.6, s32[1024]{0:T(1024)S(1)} %get-tuple-element.16), kind=kCustom, calls=%fused_computation.2.clone | custom fusion | bytes 8388624 | tf_op jit(solution)/shard_map/jit(_take)/gather | solution.py:31
  138.0 13.9 %fusion.9 = bf16[512,2,2,2,512]{4,0,3,2,1:T(8,128)(2,1)} fusion(bf16[2,512,512]{2,1,0:T(8,128)(2,1)S(1)} %copy-done, bf16[2,2,2,2,256,512]{5,4,3,2,1,0:T(8,128)(2,1)} %bitcast.96, bf16[2,2,2,2,256,512]{5,4,3,2,1,0:T(8,128)(2,1)} %bitcast.97, bf16[2,2,2,2,256,512]{5,4,3,2,1,0:T(8,128)(2,1)} %bitcast.98, bf16[2,2,2,2,256,512]{5,4,3,2,1,0:T(8,128)(2,1)} %bitcast.99, ...), kind=kOutput, calls=%fused_computation.13 | convolution fusion | flops 8663334912 | bytes 22020120 | tf_op jit(solution)/shard_map/fescrj,fkj->resck/dot_general | solution.py:44
  151.9 44.2 %reduce-scatter.2.cloned.1.call-done = bf16[128,2,2,2,512]{4,0,3,2,1:T(8,128)(2,1)} async-done(((bf16[512,2,2,2,512]{4,0,3,2,1:T(8,128)(2,1)}), bf16[128,2,2,2,512]{4,0,3,2,1:T(8,128)(2,1)}) %reduce-scatter.2.cloned.1.call-update) | async-done | bytes 1048592 | tf_op jit(solution)/shard_map/reduce_scatter | solution.py:43
  196.1 1.4 fusion.67
  197.5 1.4 collective-permute-start.3
  199.0 4.6 %collective-permute-start.2 = (bf16[128,2,1,2,512]{4,0,3,2,1:T(8,128)(2,1)S(1)}, bf16[128,2,1,2,512]{4,0,3,2,1:T(8,128)(2,1)S(1)}, u32[]{:S(2)}, u32[]{:S(2)}) collective-permute-start(bf16[128,2,1,2,512]{4,0,3,2,1:T(8,128)(2,1)S(1)} %get-tuple-element.10), channel_id=1, source_target_pairs={{0,16},{1,17},{2,18},{3,19},{4,20},{5,21},{6,22},{7,23},{8,24},{9,... | collective-permute-start | bytes 1572872 | tf_op jit(solution)/shard_map/ppermute | solution.py:15
  203.6 9.5 %collective-permute-done.3 = bf16[128,2,1,2,512]{4,0,3,2,1:T(8,128)(2,1)S(1)} collective-permute-done((bf16[128,2,1,2,512]{4,0,3,2,1:T(8,128)(2,1)S(1)}, bf16[128,2,1,2,512]{4,0,3,2,1:T(8,128)(2,1)S(1)}, u32[]{:S(2)}, u32[]{:S(2)}) %collective-permute-start.3) | collective-permute-done | bytes 524320 | tf_op jit(solution)/shard_map/ppermute | solution.py:18
  213.0 1.2 collective-permute-done.2
  214.2 2.1 add_convert_fusion.1
  216.3 0.8 fusion.14
  217.1 0.8 fusion.16
  217.9 0.8 fusion.49
  218.8 0.8 fusion.46
  219.6 1.1 pad_maximum_fusion.3
  220.7 3.9 %slice_bitcast_fusion.7 = (bf16[2,2,1,512,512]{4,3,1,0,2:T(8,128)(2,1)}, bf16[2,2,1,512,512]{4,3,1,0,2:T(8,128)(2,1)S(1)}) fusion(bf16[2,2,2,512,512]{4,3,2,1,0:T(8,128)(2,1)} %param.9), kind=kLoop, calls=%fused_computation.35 | loop fusion | bytes 8388608
  224.6 31.7 %all-gather.2.cloned.1.call-done = bf16[512,2,2,2,512]{4,0,2,1,3:T(8,128)(2,1)} async-done(((bf16[128,2,2,2,512]{4,0,2,1,3:T(8,128)(2,1)}), bf16[512,2,2,2,512]{4,0,2,1,3:T(8,128)(2,1)}) %all-gather.2.cloned.1.call-update) | async-done | bytes 4194320 | tf_op jit(solution)/shard_map/all_gather | solution.py:66
  256.3 2.2 fusion.22
  258.5 2.2 fusion.23
  260.7 1.5 fusion.33
  263.0 1.6 copy.9
  (26 shorter events, 2.4 us)
Async XLA Ops:
  6.5 131.4 %copy-start = (bf16[2,512,512]{2,1,0:T(8,128)(2,1)S(1)}, bf16[2,512,512]{2,1,0:T(8,128)(2,1)}, u32[]{:S(2)}) copy-start(bf16[2,512,512]{2,1,0:T(8,128)(2,1)} %param.10) | copy-start | bytes 3145732
  6.5 189.6 %reduce-scatter.2.cloned.1.call-start = ((), (), s32[]{:S(2)}) async-start(), calls=%async_computation.1 | async-start | bytes 5242880 | tf_op jit(solution)/shard_map/reduce_scatter | solution.py:43
  6.5 95.2 %collective-permute-start = (bf16[2,2,2,512,512]{4,3,2,1,0:T(8,128)(2,1)}, bf16[2,2,2,512,512]{4,3,2,1,0:T(8,128)(2,1)}, u32[]{:S(2)}, u32[]{:S(2)}) collective-permute-start(bf16[2,2,2,512,512]{4,3,2,1,0:T(8,128)(2,1)} %param.8), channel_id=1, source_target_pairs={{0,1},{1,2},{2,3},{4,5},{5,6},{6,7},{8,9},{9,10},{10,11},{12,13},{... | collective-permute-start | bytes 12582920 | tf_op jit(solution)/shard_map/ppermute | solution.py:15
  13.6 94.2 %collective-permute-start.1 = (bf16[2,2,2,512,512]{4,3,2,1,0:T(8,128)(2,1)}, bf16[2,2,2,512,512]{4,3,2,1,0:T(8,128)(2,1)}, u32[]{:S(2)}, u32[]{:S(2)}) collective-permute-start(bf16[2,2,2,512,512]{4,3,2,1,0:T(8,128)(2,1)} %param.8), channel_id=1, source_target_pairs={{1,0},{2,1},{3,2},{5,4},{6,5},{7,6},{9,8},{10,9},{11,10},{13,12},{... | collective-permute-start | bytes 12582920 | tf_op jit(solution)/shard_map/ppermute | solution.py:18
  17.2 87.2 %copy-start.4 = (bf16[2,2,2,512,512]{4,3,2,1,0:T(8,128)(2,1)S(1)}, bf16[2,2,2,512,512]{4,3,2,1,0:T(8,128)(2,1)}, u32[]{:S(2)}) copy-start(bf16[2,2,2,512,512]{4,3,2,1,0:T(8,128)(2,1)} %param.8) | copy-start | bytes 12582916
  132.3 5.7 %copy-start.6 = (f32[2]{0:T(128)S(1)}, f32[2]{0:T(128)}, u32[]{:S(2)}) copy-start(f32[2]{0:T(128)} %param.11) | copy-start | bytes 28
  151.8 62.4 %copy-start.5 = (f32[2]{0:T(128)S(1)}, f32[2]{0:T(128)}, u32[]{:S(2)}) copy-start(f32[2]{0:T(128)} %param.13) | copy-start | bytes 28
  151.9 104.4 %all-gather.2.cloned.1.call-start = ((), (), s32[]{:S(2)}) async-start(), calls=%async_computation.2 | async-start | bytes 5242880 | tf_op jit(solution)/shard_map/all_gather | solution.py:66
  196.1 20.2 %copy-start.2 = (bf16[2,2,2,512,512]{4,3,2,1,0:T(8,128)(2,1)S(1)}, bf16[2,2,2,512,512]{4,3,2,1,0:T(8,128)(2,1)}, u32[]{:S(2)}) copy-start(bf16[2,2,2,512,512]{4,3,2,1,0:T(8,128)(2,1)} %param.9) | copy-start | bytes 12582916
  197.5 15.5 %collective-permute-start.3 = (bf16[128,2,1,2,512]{4,0,3,2,1:T(8,128)(2,1)S(1)}, bf16[128,2,1,2,512]{4,0,3,2,1:T(8,128)(2,1)S(1)}, u32[]{:S(2)}, u32[]{:S(2)}) collective-permute-start(bf16[128,2,1,2,512]{4,0,3,2,1:T(8,128)(2,1)S(1)} %get-tuple-element.11), channel_id=1, source_target_pairs={{16,0},{17,1},{18,2},{19,3},{20,4},{21,5},{22,6},{23,7},{24,8},{25... | collective-permute-start | bytes 1572872 | tf_op jit(solution)/shard_map/ppermute | solution.py:18
  199.0 15.3 %collective-permute-start.2 = (bf16[128,2,1,2,512]{4,0,3,2,1:T(8,128)(2,1)S(1)}, bf16[128,2,1,2,512]{4,0,3,2,1:T(8,128)(2,1)S(1)}, u32[]{:S(2)}, u32[]{:S(2)}) collective-permute-start(bf16[128,2,1,2,512]{4,0,3,2,1:T(8,128)(2,1)S(1)} %get-tuple-element.10), channel_id=1, source_target_pairs={{0,16},{1,17},{2,18},{3,19},{4,20},{5,21},{6,22},{7,23},{8,24},{9,... | collective-permute-start | bytes 1572872 | tf_op jit(solution)/shard_map/ppermute | solution.py:15
  256.3 4.4 %copy-start.3 = (bf16[512,2,2,2,512]{4,0,2,1,3:T(8,128)(2,1)S(1)}, bf16[512,2,2,2,512]{4,0,2,1,3:T(8,128)(2,1)}, u32[]{:S(2)}) copy-start(bf16[512,2,2,2,512]{4,0,2,1,3:T(8,128)(2,1)} %all-gather.2.cloned.1.call-done) | copy-start | bytes 12582916
  262.3 2.3 copy-start.1
Sparse Core Ops, SparseCore 0:
  152.0 44.0 reduce-scatter.1
  220.8 35.4 all-gather.1
where the time goes:
time: 272 us; the launch traced here: 271 us
  waiting for transfers between devices  174 us (64%)
  local copies, waits for them, and re-layouts  40.6 us (15%)
  matrix products  23.5 us (9%)
  starting transfers between devices  14.4 us (5%)
  between operations  13.6 us (5%)
  other arithmetic  5.53 us (2%)
    ppermute x2, waiting for transfers between devices, with_halo(): lax.ppermute(lax.slice_in_dim(block, block.shape[dim] - width, None, axis...  85.8 us
    reduce_scatter x1, waiting for transfers between devices, shards(): lax.psum_scatter(jnp.einsum('fescrj,fkj->resck', left_product, coupling,...  44.2 us
    all_gather x1, waiting for transfers between devices, shards(): y_piece = lax.all_gather(product, 'freq', axis=0, tiled=True)  31.7 us
    gather x3, local copies, waits for them, and re-layouts, shards(): lower_green = jnp.take(padded, positions - offsets[:, None], axis=0)  16.2 us
    dot_general x1, matrix products, shards(): jnp.einsum('fescrj,fkj->resck', left_product, coupling, preferred_element...  13.9 us
    ppermute x2, waiting for transfers between devices, with_halo(): lax.ppermute(lax.slice_in_dim(block, 0, width, axis=dim), axis, backward)  12.1 us
    ppermute x2, starting transfers between devices, with_halo(): lax.ppermute(lax.slice_in_dim(block, block.shape[dim] - width, None, axis...  11.6 us
    gather x2, local copies, waits for them, and re-layouts, shards(): upper_green = jnp.take(padded, positions + offsets[:, None], axis=0)  11.2 us
  transfers between devices with their start and end apart: 6, of which 6 were waited for; matrix products, arithmetic and copies ran while one was open for 4% of the time, Pallas kernels for 0%

commit v1 on v0

v1 whole, which is shorter than its diff:
```python
import functools
import jax
import jax.numpy as jnp
from jax import lax
from jax.experimental import pallas as pl
from jax.experimental.pallas import tpu as pltpu
from jax.sharding import PartitionSpec as P

OFFMAX = 2
MESH = pl.DeviceIdType.MESH
F32 = jnp.float32
BF16 = jnp.bfloat16


def with_halo(block, sides, width):
    for axis, dim in sides:
        count = lax.axis_size(axis)
        forward = [(i, i + 1) for i in range(count - 1)]
        backward = [(target, source) for source, target in forward]
        low = lax.ppermute(
            lax.slice_in_dim(block, block.shape[dim] - width, None, axis=dim), axis, forward
        )
        high = lax.ppermute(lax.slice_in_dim(block, 0, width, axis=dim), axis, backward)
        block = jnp.concatenate([low, block, high], axis=dim)
    return block


def general(lesser, retarded, coupling, occupations, offsets, intersection):
    freq_count = lax.axis_size("freq")
    row_count = lesser.shape[-1] // freq_count
    row_first = lax.axis_index("freq") * row_count
    padded = with_halo(lesser, (("energy", 0),), OFFMAX)
    energy_count = lesser.shape[0]
    positions = jnp.arange(energy_count, dtype=jnp.int32)[None, :] + OFFMAX
    lower_green = jnp.take(padded, positions - offsets[:, None], axis=0)
    upper_green = jnp.take(padded, positions + offsets[:, None], axis=0)
    scale = occupations[:, None, None, None, None, None]
    mixture = (
        scale * lower_green.astype(F32) + (scale + 1.0) * upper_green.astype(F32)
    ).astype(BF16)
    real_green = retarded[:, :, 0]
    imag_green = retarded[:, :, 1]
    real_rows = lax.dynamic_slice_in_dim(real_green, row_first, row_count, 2)
    imag_rows = lax.dynamic_slice_in_dim(imag_green, row_first, row_count, 2)
    left_product = jnp.einsum(
        "fri,fescij->fescrj", coupling, mixture, preferred_element_type=F32
    ).astype(BF16)
    self_energy = lax.psum_scatter(
        jnp.einsum(
            "fescrj,fkj->resck", left_product, coupling, preferred_element_type=F32
        ).astype(BF16),
        "freq",
        scatter_dimension=0,
        tiled=True,
    )
    beside_all = with_halo(self_energy, (("slab", 2),), 1)
    beside = beside_all[:, :, :-2].astype(F32) + beside_all[:, :, 2:].astype(F32)
    total = self_energy.astype(F32) + intersection[None, None, :, None, None] * beside
    combined = total.astype(BF16)
    real_self = combined[:, :, :, 0]
    imag_self = combined[:, :, :, 1]

    def by_transpose(left_side, right_side):
        return jnp.einsum("resj,eskj->resk", left_side, right_side, preferred_element_type=F32)

    real_part = by_transpose(real_self, real_green) + by_transpose(imag_self, imag_green)
    imag_part = by_transpose(imag_self, real_green) - by_transpose(real_self, imag_green)
    product = jnp.stack([real_part, imag_part], axis=3).astype(BF16)
    y_piece = lax.all_gather(product, "freq", axis=0, tiled=True)
    real_piece = y_piece[:, :, :, 0]
    imag_piece = y_piece[:, :, :, 1]

    def plain_product(left_side, right_side):
        return jnp.einsum("esrm,mesk->esrk", left_side, right_side, preferred_element_type=F32)

    out_real = plain_product(real_rows, real_piece) - plain_product(imag_rows, imag_piece)
    out_imag = plain_product(real_rows, imag_piece) + plain_product(imag_rows, real_piece)
    return jnp.stack([out_real, out_imag], axis=2)


def by_rows(a, b):
    return lax.dot_general(a, b, (((1,), (1,)), ((), ())), preferred_element_type=F32)


def kernel(
    chunks, slabs, energies,
    lesser, retarded, coupling, weights, beside_weight, out,
    own, low, high, c_buf, w_buf, r_buf, acc, half, near, far, comb,
    local_sem, send_sem, recv_sem,
):
    nf, size, _ = coupling.shape
    cut = size // chunks
    x, q, z = lax.axis_index("slab"), lax.axis_index("freq"), lax.axis_index("energy")
    y, core = q // 2, q % 2
    partner = {"freq": 2 * y + 1 - core}
    across = {"freq": 2 * (1 - y) + core}
    diagonal = {"freq": 2 * (1 - y) + 1 - core}
    has_low, has_high = z > 0, z < energies - 1
    below = {"energy": jnp.maximum(z - 1, 0)}
    above = {"energy": jnp.minimum(z + 1, energies - 1)}
    x_to = x + 2 * core - 1
    has_x = jnp.logical_and(x_to >= 0, x_to < slabs)
    beside = {"slab": jnp.clip(x_to, 0, slabs - 1), "freq": 2 * y + 1 - core}

    barrier = pltpu.get_barrier_semaphore()
    peers = [(None, partner), (None, across), (None, diagonal), (has_low, below), (has_high, above), (has_x, beside)]

    def under(condition, action):
        if condition is None:
            action()
        else:
            pl.when(condition)(action)

    for condition, peer in peers:
        under(condition, lambda peer=peer: pl.semaphore_signal(barrier, inc=1, device_id=peer, device_id_type=MESH))

    count = [0]

    def remote(src, dst, peer):
        n = count[0]
        count[0] += 1
        return pltpu.make_async_remote_copy(
            src_ref=src, dst_ref=dst, send_sem=send_sem.at[n], recv_sem=recv_sem.at[n],
            device_id=peer, device_id_type=MESH,
        )

    load_own = pltpu.make_async_copy(lesser.at[:, core, y], own, local_sem.at[0])
    load_c = pltpu.make_async_copy(coupling, c_buf.at[pl.ds(0, nf)], local_sem.at[1])
    load_w = pltpu.make_async_copy(weights, w_buf.at[pl.ds(0, nf)], local_sem.at[2])
    load_r = pltpu.make_async_copy(retarded, r_buf, local_sem.at[3])
    for load in (load_own, load_c, load_w, load_r):
        load.start()

    def zero(ref):
        ref[...] = jnp.zeros_like(ref)

    pl.when(jnp.logical_not(has_low))(lambda: zero(low))
    pl.when(jnp.logical_not(has_high))(lambda: zero(high))
    pl.when(jnp.logical_not(has_x))(lambda: zero(far))
    zero(acc)

    greeted = 3 + sum(condition.astype(jnp.int32) for condition in (has_low, has_high, has_x))
    pl.semaphore_wait(barrier, greeted)

    sent = []

    def go(copy, condition=None):
        under(condition, copy.start)
        sent.append((condition, copy))
        return copy

    w_in = [
        go(remote(weights, w_buf.at[pl.ds(slot * nf, nf)], peer))
        for slot, peer in ((1, partner), (2, across), (3, diagonal))
    ]
    ups, downs, c_across = [], [], []
    c_near = [go(remote(coupling.at[i], c_buf.at[nf + i], partner)) for i in range(nf)]
    for k in range(chunks):
        columns = pl.ds(k * cut, cut)
        ups.append(go(remote(lesser.at[:, core, y, :, columns], low.at[k], above), has_high))
        downs.append(go(remote(lesser.at[:, core, y, :, columns], high.at[k], below), has_low))
        if k == 0:
            c_across = [go(remote(coupling.at[i], c_buf.at[2 * nf + i], across)) for i in range(nf)]

    load_own.wait()
    load_c.wait()
    load_w.wait()
    for copy in w_in:
        copy.wait_recv()

    def terms(k, e):
        columns = slice(k * cut, (k + 1) * cut)
        if e == 0:
            return low.at[k, 1], low.at[k, 0], own.at[1, :, columns], high.at[k, 0]
        return own.at[0, :, columns], low.at[k, 1], high.at[k, 0], high.at[k, 1]

    def sandwich(k, e, first, last):
        columns = slice(k * cut, (k + 1) * cut)
        refs = terms(k, e)

        def body(f, carry):
            w = w_buf[f]
            mixed = w[0:1] * refs[0][...].astype(F32)
            for i in (1, 2, 3):
                mixed = mixed + w[i : i + 1] * refs[i][...].astype(F32)
            left = jnp.dot(c_buf[f], mixed.astype(BF16), preferred_element_type=F32).astype(BF16)
            acc[e] += by_rows(left, c_buf[f, :, columns])
            return carry

        lax.fori_loop(first, last, body, 0)

    def arrive(k):
        pl.when(has_low)(ups[k].wait_recv)
        pl.when(has_high)(downs[k].wait_recv)

    arrive(0)
    for copy in c_near:
        copy.wait_recv()
    sandwich(0, 0, 0, 2 * nf)
    sandwich(0, 1, 0, 2 * nf)
    c_far = []
    for i in range(nf):
        c_across[i].wait_recv()
        c_far.append(go(remote(c_buf.at[2 * nf + i], c_buf.at[3 * nf + i], partner)))
    for copy in c_far:
        copy.wait_recv()
    for e in range(2):
        sandwich(0, e, 2 * nf, 4 * nf)

    to_near, to_far = [], []

    def finish_self(e):
        half[e] = acc[e].astype(BF16)
        to_far.append(go(remote(half.at[e], far.at[e], beside), has_x))
        to_near.append(go(remote(half.at[e], near.at[e], partner)))

    for k in range(1, chunks):
        arrive(k)
        for e in range(2):
            sandwich(k, e, 0, 4 * nf)
            if k == chunks - 1:
                finish_self(e)

    comb_near, comb_across = [], []
    for e in range(2):
        to_near[e].wait_recv()
        pl.when(has_x)(to_far[e].wait_recv)
        around = near[e].astype(F32) + far[e].astype(F32)
        comb[e, 0] = (half[e].astype(F32) + beside_weight[core] * around).astype(BF16)
        comb_across.append(go(remote(comb.at[e, 0], comb.at[e, 2], across)))
        comb_near.append(go(remote(comb.at[e, 0], comb.at[e, 1], partner)))

    load_r.wait()
    rows = size // 4
    mine = pl.ds(pl.multiple_of(q * rows, rows), rows)
    for e in range(2):
        comb_near[e].wait_recv()
        comb_across[e].wait_recv()
        comb_far = go(remote(comb.at[e, 2], comb.at[e, 3], partner))
        for other in range(2):
            if other == 1:
                comb_far.wait_recv()
            s = core if other == 0 else 1 - core
            edge = jnp.concatenate([r_buf[e, s, 0, mine, :], r_buf[e, s, 1, mine, :]], axis=0)
            with_real = jnp.dot(edge, comb[e, 2 * y + other], preferred_element_type=F32)
            with_imag = jnp.dot(edge, comb[e, 2 * (1 - y) + other], preferred_element_type=F32)
            middle = jnp.concatenate(
                [with_real[:rows] - with_imag[rows:], with_imag[:rows] + with_real[rows:]], axis=0
            ).astype(BF16)
            by_real = by_rows(middle, r_buf[e, s, 0])
            by_imag = by_rows(middle, r_buf[e, s, 1])
            out[e, s, 0] = by_real[:rows] + by_imag[rows:]
            out[e, s, 1] = by_real[rows:] - by_imag[:rows]

    for condition, copy in sent:
        under(condition, copy.wait_send)


def fast(lesser, retarded, coupling, occupations, offsets, intersection):
    nf, size, _ = coupling.shape
    chunks = 2
    cut = size // chunks
    near = (offsets == 1).astype(F32)
    away = (offsets == 2).astype(F32)
    more = occupations + 1.0
    rows = jnp.stack([occupations * near, occupations * away, more * near, more * away], axis=1)
    weights = jnp.broadcast_to(jnp.tile(rows, (1, 2))[:, :, None], (nf, 8, cut))
    copies = 3 + 2 * nf + nf + 2 * chunks + 4 + 4 + 2
    anywhere = pl.BlockSpec(memory_space=pl.ANY)
    return pl.pallas_call(
        functools.partial(kernel, chunks, lax.axis_size("slab"), lax.axis_size("energy")),
        out_shape=jax.ShapeDtypeStruct((2, 2, 2, size // 4, size), F32),
        in_specs=[anywhere] * 4 + [pl.BlockSpec(memory_space=pltpu.SMEM)],
        out_specs=pl.BlockSpec(memory_space=pltpu.VMEM),
        scratch_shapes=[
            pltpu.VMEM((2, size, size), BF16),
            pltpu.VMEM((chunks, 2, size, cut), BF16),
            pltpu.VMEM((chunks, 2, size, cut), BF16),
            pltpu.VMEM((4 * nf, size, size), BF16),
            pltpu.VMEM((4 * nf, 8, cut), F32),
            pltpu.VMEM((2, 2, 2, size, size), BF16),
            pltpu.VMEM((2, size, size), F32),
            pltpu.VMEM((2, size, size), BF16),
            pltpu.VMEM((2, size, size), BF16),
            pltpu.VMEM((2, size, size), BF16),
            pltpu.VMEM((2, 4, size, size), BF16),
            pltpu.SemaphoreType.DMA((4,)),
            pltpu.SemaphoreType.DMA((copies,)),
            pltpu.SemaphoreType.DMA((copies,)),
        ],
        compiler_params=pltpu.CompilerParams(
            collective_id=0, has_side_effects=True, vmem_limit_bytes=60 << 20
        ),
    )(lesser, retarded, coupling, weights, intersection)


def solution(mesh):
    def shards(lesser, retarded, *rest):
        fits = (
            mesh.shape["freq"] == 4
            and lesser.shape[:2] == (2, 2)
            and lesser.shape[-1] % 512 == 0
            and rest[0].shape[0] * lesser.shape[-1] <= 1024
        )
        return (fast if fits else general)(lesser, retarded, *rest)

    return jax.shard_map(
        shards,
        mesh=mesh,
        in_specs=(
            P("energy", "slab", None, None, None),
            P("energy", "slab", None, None, None),
            P("freq", None, None),
            P("freq"),
            P("freq"),
            P("slab"),
        ),
        out_specs=P("energy", "slab", None, "freq", None),
        check_vma=False,
    )
```

time: 272 us -> 81.9 us (0.30)
  waiting for transfers between devices: 174 us -> 0 us
  Pallas kernels: 0 us -> 77.1 us
  local copies, waits for them, and re-layouts: 40.6 us -> 3.94 us
  matrix products: 23.5 us -> 0 us
  starting transfers between devices: 14.4 us -> 0 us
  between operations: 13.6 us -> 0.01 us
  other arithmetic: 5.53 us -> 0.69 us
    ppermute x4 -> x0, waiting for transfers between devices: 97.9 us -> none  [the longest x2 85.8 us: with_halo(): lax.ppermute(lax.slice_in_dim(block, block.shape[dim] - width, None, axis...]
    pallas_call x0 -> x1, Pallas kernels: none -> 77.1 us  [fast(): pl.pallas_call(functools.partial(kernel, chunks, lax.axis_size('slab'), l...]
    reduce_scatter x1 -> x0, waiting for transfers between devices: 44.2 us -> none  [shards(): lax.psum_scatter(jnp.einsum('fescrj,fkj->resck', left_product, coupling,...]
    all_gather x1 -> x0, waiting for transfers between devices: 31.7 us -> none  [shards(): y_piece = lax.all_gather(product, 'freq', axis=0, tiled=True)]
    gather x5 -> x0, local copies, waits for them, and re-layouts: 27.4 us -> none  [the longest x3 16.2 us: shards(): lower_green = jnp.take(padded, positions - offsets[:, None], axis=0)]
    dot_general x9 -> x0, matrix products: 23.5 us -> none  [the longest x1 13.9 us: shards(): jnp.einsum('fescrj,fkj->resck', left_product, coupling, preferred_element...]
    ppermute x4 -> x0, starting transfers between devices: 14.3 us -> none  [the longest x2 11.6 us: with_halo(): lax.ppermute(lax.slice_in_dim(block, block.shape[dim] - width, None, axis...]
    unnamed x17 -> x1, local copies, waits for them, and re-layouts: 7.36 us -> 3.08 us
  transfers between devices with their start and end apart: 6 -> 0, of which waited for: 6 -> 0; matrix products, arithmetic and copies ran while one was open for 4% -> 0% of each run, Pallas kernels for 0% -> 0%
where the time goes in v1:
time: 81.9 us; the launch traced here: 81.7 us
  Pallas kernels  77.1 us (94%)
  local copies, waits for them, and re-layouts  3.94 us (5%)
    pallas_call x1, Pallas kernels, fast(): pl.pallas_call(functools.partial(kernel, chunks, lax.axis_size('slab'), l...  77.1 us
    unnamed x1, local copies, waits for them, and re-layouts  3.08 us

profile of v1, /device:TPU:0, one launch (start us, length us, event | category | flops | bytes accessed | tf_op | source)
XLA Modules:
  0.0 81.7 jit_solution(14284503139530278496)
XLA Ops:
  0.0 0.7 fusion
  0.7 0.1 copy.7
  0.8 0.1 tile.9
  0.9 0.7 broadcast_in_dim.2.weights
  1.6 77.1 %shard_map.64 = f32[2,2,2,128,512]{4,3,2,1,0:T(8,128)} custom-call(bf16[2,2,2,512,512]{4,3,2,1,0:T(8,128)(2,1)} %lesser.1, bf16[2,2,2,512,512]{4,3,2,1,0:T(8,128)(2,1)} %retarded.1, bf16[2,512,512]{2,1,0:T(8,128)(2,1)} %coupling.1, f32[2,8,256]{2,1,0:T(8,128)} %broadcast_in_dim.2.weights, f32[2]{0:T(128)} %beside_weight.1), custom_call_target="tpu_custom_call" | custom-call | tf_op jit(solution)/shard_map/pallas_call | solution.py:270
  78.6 3.1 %copy.9 = f32[2,2,2,128,512]{4,3,2,1,0:T(8,128)} copy(f32[2,2,2,128,512]{4,3,2,1,0:T(8,128)} %shard_map.64) | data formatting | bytes 4194304
  (2 shorter events, 0.0 us)

commit v2 on v1

--- a/solution.py
+++ b/solution.py
@@ -7,6 +7,7 @@
 from jax.sharding import PartitionSpec as P
 
 OFFMAX = 2
+UNROLL = 4
 MESH = pl.DeviceIdType.MESH
 F32 = jnp.float32
 BF16 = jnp.bfloat16
@@ -84,8 +85,8 @@
 
 def kernel(
     chunks, slabs, energies,
-    lesser, retarded, coupling, weights, beside_weight, out,
-    own, low, high, c_buf, w_buf, r_buf, acc, half, near, far, comb,
+    lesser, retarded, coupling, numbers, shifts, beside_weight, out,
+    own, low, high, c_buf, w_buf, r_buf, left_buf, acc, half, near, far, comb,
     local_sem, send_sem, recv_sem,
 ):
     nf, size, _ = coupling.shape
@@ -95,6 +96,7 @@
     partner = {"freq": 2 * y + 1 - core}
     across = {"freq": 2 * (1 - y) + core}
     diagonal = {"freq": 2 * (1 - y) + 1 - core}
+    opposite = {"slab": 1 - x}
     has_low, has_high = z > 0, z < energies - 1
     below = {"energy": jnp.maximum(z - 1, 0)}
     above = {"energy": jnp.minimum(z + 1, energies - 1)}
@@ -103,7 +105,7 @@
     beside = {"slab": jnp.clip(x_to, 0, slabs - 1), "freq": 2 * y + 1 - core}
 
     barrier = pltpu.get_barrier_semaphore()
-    peers = [(None, partner), (None, across), (None, diagonal), (has_low, below), (has_high, above), (has_x, beside)]
+    peers = [(None, partner), (None, across), (None, diagonal), (None, opposite), (has_low, below), (has_high, above), (has_x, beside)]
 
     def under(condition, action):
         if condition is None:
@@ -125,11 +127,30 @@
         )
 
     load_own = pltpu.make_async_copy(lesser.at[:, core, y], own, local_sem.at[0])
-    load_c = pltpu.make_async_copy(coupling, c_buf.at[pl.ds(0, nf)], local_sem.at[1])
-    load_w = pltpu.make_async_copy(weights, w_buf.at[pl.ds(0, nf)], local_sem.at[2])
-    load_r = pltpu.make_async_copy(retarded, r_buf, local_sem.at[3])
-    for load in (load_own, load_c, load_w, load_r):
+    load_c = [
+        pltpu.make_async_copy(
+            coupling.at[i, :, pl.ds(k * cut, cut)],
+            c_buf.at[k, :, pl.ds(i * cut, cut)],
+            local_sem.at[3 + i * chunks + k],
+        )
+        for i in range(nf)
+        for k in range(chunks)
+    ]
+    load_r = pltpu.make_async_copy(retarded, r_buf, local_sem.at[1])
+    for load in [load_own, load_r] + load_c:
         load.start()
+
+    for i in range(nf):
+        number, shift = numbers[i], shifts[i]
+        none = jnp.float32(0.0)
+        row = [
+            jnp.where(shift == 1, number, none),
+            jnp.where(shift == 2, number, none),
+            jnp.where(shift == 1, number + 1.0, none),
+            jnp.where(shift == 2, number + 1.0, none),
+        ]
+        for j in range(8):
+            w_buf[i, j : j + 1, :] = jnp.full((1, cut), row[j % 4], F32)
 
     def zero(ref):
         ref[...] = jnp.zeros_like(ref)
@@ -137,9 +158,8 @@
     pl.when(jnp.logical_not(has_low))(lambda: zero(low))
     pl.when(jnp.logical_not(has_high))(lambda: zero(high))
     pl.when(jnp.logical_not(has_x))(lambda: zero(far))
-    zero(acc)
-
-    greeted = 3 + sum(condition.astype(jnp.int32) for condition in (has_low, has_high, has_x))
+
+    greeted = 4 + sum(condition.astype(jnp.int32) for condition in (has_low, has_high, has_x))
     pl.semaphore_wait(barrier, greeted)
 
     sent = []
@@ -150,21 +170,28 @@
         return copy
 
     w_in = [
-        go(remote(weights, w_buf.at[pl.ds(slot * nf, nf)], peer))
+        go(remote(w_buf.at[pl.ds(0, nf)], w_buf.at[pl.ds(slot * nf, nf)], peer))
         for slot, peer in ((1, partner), (2, across), (3, diagonal))
     ]
-    ups, downs, c_across = [], [], []
-    c_near = [go(remote(coupling.at[i], c_buf.at[nf + i], partner)) for i in range(nf)]
+
+    def part(slot, k):
+        start = slot * cut
+        return c_buf.at[k, :, pl.ds(start if isinstance(start, int) else pl.multiple_of(start, cut), cut)]
+
+    ups, downs, c_across, c_near = [], [], [], []
     for k in range(chunks):
         columns = pl.ds(k * cut, cut)
+        c_across.append(go(remote(coupling.at[x, :, columns], part(2 * nf + x, k), across)))
+    for k in range(chunks):
+        columns = pl.ds(k * cut, cut)
+        for i in range(nf):
+            c_near.append(go(remote(coupling.at[i, :, columns], part(nf + i, k), partner)))
         ups.append(go(remote(lesser.at[:, core, y, :, columns], low.at[k], above), has_high))
         downs.append(go(remote(lesser.at[:, core, y, :, columns], high.at[k], below), has_low))
-        if k == 0:
-            c_across = [go(remote(coupling.at[i], c_buf.at[2 * nf + i], across)) for i in range(nf)]
 
     load_own.wait()
-    load_c.wait()
-    load_w.wait()
+    for load in load_c:
+        load.wait()
     for copy in w_in:
         copy.wait_recv()
 
@@ -174,73 +201,109 @@
             return low.at[k, 1], low.at[k, 0], own.at[1, :, columns], high.at[k, 0]
         return own.at[0, :, columns], low.at[k, 1], high.at[k, 0], high.at[k, 1]
 
-    def sandwich(k, e, first, last):
-        columns = slice(k * cut, (k + 1) * cut)
+    def left_side(k, e, number, slot_of):
         refs = terms(k, e)
 
-        def body(f, carry):
+        def body(j, carry):
+            f = slot_of(j)
             w = w_buf[f]
             mixed = w[0:1] * refs[0][...].astype(F32)
             for i in (1, 2, 3):
                 mixed = mixed + w[i : i + 1] * refs[i][...].astype(F32)
-            left = jnp.dot(c_buf[f], mixed.astype(BF16), preferred_element_type=F32).astype(BF16)
-            acc[e] += by_rows(left, c_buf[f, :, columns])
+            columns = pl.ds(pl.multiple_of(f * cut, cut), cut)
+            whole = jnp.concatenate([c_buf[h, :, columns] for h in range(chunks)], axis=1)
+            left = jnp.dot(whole, mixed.astype(BF16), preferred_element_type=F32)
+            left_buf[e, :, columns] = left.astype(BF16)
             return carry
 
-        lax.fori_loop(first, last, body, 0)
+        lax.fori_loop(0, number, body, 0, unroll=UNROLL)
+
+    def right_side(k, e):
+        return by_rows(left_buf[e], c_buf[k])
 
     def arrive(k):
         pl.when(has_low)(ups[k].wait_recv)
         pl.when(has_high)(downs[k].wait_recv)
 
+    relayed, c_far = [], []
+    for k in range(chunks):
+        c_across[k].wait_recv()
+        relayed.append(go(remote(part(2 * nf + x, k), part(2 * nf + x, k), opposite)))
+        c_far.append(go(remote(part(2 * nf + x, k), part(3 * nf + x, k), partner)))
     arrive(0)
     for copy in c_near:
         copy.wait_recv()
-    sandwich(0, 0, 0, 2 * nf)
-    sandwich(0, 1, 0, 2 * nf)
-    c_far = []
-    for i in range(nf):
-        c_across[i].wait_recv()
-        c_far.append(go(remote(c_buf.at[2 * nf + i], c_buf.at[3 * nf + i], partner)))
-    for copy in c_far:
+    for e in range(2):
+        left_side(0, e, 2 * nf, lambda j: j)
+    other_x = 1 - x
+    c_rest = []
+    for k in range(chunks):
+        relayed[k].wait_recv()
+        c_rest.append(go(remote(part(2 * nf + other_x, k), part(3 * nf + other_x, k), partner)))
+    for copy in c_far + c_rest:
         copy.wait_recv()
     for e in range(2):
-        sandwich(0, e, 2 * nf, 4 * nf)
+        left_side(0, e, 2 * nf, lambda j: 2 * nf + j)
+        acc[e] = right_side(0, e)
 
     to_near, to_far = [], []
 
     def finish_self(e):
-        half[e] = acc[e].astype(BF16)
+        half[e] = (acc[e] + right_side(chunks - 1, e)).astype(BF16)
         to_far.append(go(remote(half.at[e], far.at[e], beside), has_x))
         to_near.append(go(remote(half.at[e], near.at[e], partner)))
 
-    for k in range(1, chunks):
+    for k in range(1, chunks - 1):
         arrive(k)
         for e in range(2):
-            sandwich(k, e, 0, 4 * nf)
-            if k == chunks - 1:
-                finish_self(e)
-
-    comb_near, comb_across = [], []
-    for e in range(2):
+            left_side(k, e, 4 * nf, lambda j: j)
+            acc[e] += right_side(k, e)
+
+    comb_across = [remote(comb.at[e, 0], comb.at[e, 2], across) for e in range(2)]
+    comb_near = [remote(comb.at[e, 0], comb.at[e, 1], partner) for e in range(2)]
+    comb_far = [remote(comb.at[e, 2], comb.at[e, 3], partner) for e in range(2)]
+
+    def combine(e, with_far):
         to_near[e].wait_recv()
-        pl.when(has_x)(to_far[e].wait_recv)
-        around = near[e].astype(F32) + far[e].astype(F32)
+        around = near[e].astype(F32)
+        if with_far:
+            to_far[e].wait_recv()
+            around = around + far[e].astype(F32)
         comb[e, 0] = (half[e].astype(F32) + beside_weight[core] * around).astype(BF16)
-        comb_across.append(go(remote(comb.at[e, 0], comb.at[e, 2], across)))
-        comb_near.append(go(remote(comb.at[e, 0], comb.at[e, 1], partner)))
+        comb_across[e].start()
+        comb_near[e].start()
+
+    alone = jnp.logical_not(has_x)
+    last = chunks - 1
+    arrive(last)
+    left_side(last, 0, 4 * nf, lambda j: j)
+    finish_self(0)
+    left_side(last, 1, 4 * nf, lambda j: j)
+    pl.when(alone)(lambda: combine(0, False))
+    finish_self(1)
+    pl.when(alone)(lambda: combine(1, False))
+    pl.when(has_x)(lambda: combine(0, True))
+    pl.when(has_x)(lambda: combine(1, True))
 
     load_r.wait()
     rows = size // 4
     mine = pl.ds(pl.multiple_of(q * rows, rows), rows)
-    for e in range(2):
+
+    def pass_on(e):
+        comb_across[e].wait_recv()
+        comb_far[e].start()
+
+    def take(e):
         comb_near[e].wait_recv()
-        comb_across[e].wait_recv()
-        comb_far = go(remote(comb.at[e, 2], comb.at[e, 3], partner))
-        for other in range(2):
-            if other == 1:
-                comb_far.wait_recv()
-            s = core if other == 0 else 1 - core
+        comb_far[e].wait_recv()
+
+    for group in range(2):
+        same = alone if group == 0 else has_x
+        s = x if group == 0 else 1 - x
+        other = jnp.where(same, 0, 1)
+        for e in range(2):
+            pl.when(same)(lambda e=e: pass_on(e))
+            pl.when(jnp.logical_not(same))(lambda e=e: take(e))
             edge = jnp.concatenate([r_buf[e, s, 0, mine, :], r_buf[e, s, 1, mine, :]], axis=0)
             with_real = jnp.dot(edge, comb[e, 2 * y + other], preferred_element_type=F32)
             with_imag = jnp.dot(edge, comb[e, 2 * (1 - y) + other], preferred_element_type=F32)
@@ -252,6 +315,8 @@
             out[e, s, 0] = by_real[:rows] + by_imag[rows:]
             out[e, s, 1] = by_real[rows:] - by_imag[:rows]
 
+    for copy in comb_across + comb_near + comb_far:
+        copy.wait_send()
     for condition, copy in sent:
         under(condition, copy.wait_send)
 
@@ -260,47 +325,43 @@
     nf, size, _ = coupling.shape
     chunks = 2
     cut = size // chunks
-    near = (offsets == 1).astype(F32)
-    away = (offsets == 2).astype(F32)
-    more = occupations + 1.0
-    rows = jnp.stack([occupations * near, occupations * away, more * near, more * away], axis=1)
-    weights = jnp.broadcast_to(jnp.tile(rows, (1, 2))[:, :, None], (nf, 8, cut))
-    copies = 3 + 2 * nf + nf + 2 * chunks + 4 + 4 + 2
+    copies = 3 + (nf + 6) * chunks + 10
     anywhere = pl.BlockSpec(memory_space=pl.ANY)
     return pl.pallas_call(
         functools.partial(kernel, chunks, lax.axis_size("slab"), lax.axis_size("energy")),
         out_shape=jax.ShapeDtypeStruct((2, 2, 2, size // 4, size), F32),
-        in_specs=[anywhere] * 4 + [pl.BlockSpec(memory_space=pltpu.SMEM)],
+        in_specs=[anywhere] * 3 + [pl.BlockSpec(memory_space=pltpu.SMEM)] * 3,
         out_specs=pl.BlockSpec(memory_space=pltpu.VMEM),
         scratch_shapes=[
             pltpu.VMEM((2, size, size), BF16),
             pltpu.VMEM((chunks, 2, size, cut), BF16),
             pltpu.VMEM((chunks, 2, size, cut), BF16),
-            pltpu.VMEM((4 * nf, size, size), BF16),
+            pltpu.VMEM((chunks, size, 4 * nf * cut), BF16),
             pltpu.VMEM((4 * nf, 8, cut), F32),
             pltpu.VMEM((2, 2, 2, size, size), BF16),
+            pltpu.VMEM((2, size, 4 * nf * cut), BF16),
             pltpu.VMEM((2, size, size), F32),
             pltpu.VMEM((2, size, size), BF16),
             pltpu.VMEM((2, size, size), BF16),
             pltpu.VMEM((2, size, size), BF16),
             pltpu.VMEM((2, 4, size, size), BF16),
-            pltpu.SemaphoreType.DMA((4,)),
+            pltpu.SemaphoreType.DMA((3 + nf * chunks,)),
             pltpu.SemaphoreType.DMA((copies,)),
             pltpu.SemaphoreType.DMA((copies,)),
         ],
         compiler_params=pltpu.CompilerParams(
             collective_id=0, has_side_effects=True, vmem_limit_bytes=60 << 20
         ),
-    )(lesser, retarded, coupling, weights, intersection)
+    )(lesser, retarded, coupling, occupations, offsets, intersection)
 
 
 def solution(mesh):
     def shards(lesser, retarded, *rest):
         fits = (
-            mesh.shape["freq"] == 4
+            (mesh.shape["slab"], mesh.shape["freq"]) == (2, 4)
             and lesser.shape[:2] == (2, 2)
-            and lesser.shape[-1] % 512 == 0
-            and rest[0].shape[0] * lesser.shape[-1] <= 1024
+            and lesser.shape[-1] == 512
+            and rest[0].shape[0] == 2
         )
         return (fast if fits else general)(lesser, retarded, *rest)
 

time: 81.9 us -> 67.8 us (0.83)
  Pallas kernels: 77.1 us -> 64.6 us
  local copies, waits for them, and re-layouts: 3.94 us -> 3.08 us
    pallas_call x1, Pallas kernels: 77.1 us -> 64.6 us  [fast(): pl.pallas_call(functools.partial(kernel, chunks, lax.axis_size('slab'), l...]
where the time goes in v2:
time: 67.8 us; the launch traced here: 67.7 us
  Pallas kernels  64.6 us (95%)
  local copies, waits for them, and re-layouts  3.08 us (5%)
    pallas_call x1, Pallas kernels, fast(): pl.pallas_call(functools.partial(kernel, chunks, lax.axis_size('slab'), l...  64.6 us
    unnamed x1, local copies, waits for them, and re-layouts  3.08 us

profile of v2, /device:TPU:0, one launch (start us, length us, event | category | flops | bytes accessed | tf_op | source)
XLA Modules:
  0.0 67.7 jit_solution(12785054634146780407)
XLA Ops:
  0.0 64.6 %shard_map.64 = f32[2,2,2,128,512]{4,3,2,1,0:T(8,128)} custom-call(bf16[2,2,2,512,512]{4,3,2,1,0:T(8,128)(2,1)} %lesser.1, bf16[2,2,2,512,512]{4,3,2,1,0:T(8,128)(2,1)} %retarded.1, bf16[2,512,512]{2,1,0:T(8,128)(2,1)} %coupling.1, f32[2]{0:T(128)} %numbers.1, s32[2]{0:T(128)} %shifts.1, f32[2]{0:T(128)} %beside_weight.1), custom_call_target="tpu_custom_call" | custom-call | tf_op jit(solution)/shard_map/pallas_call | solution.py:330
  64.6 3.1 %copy.8 = f32[2,2,2,128,512]{4,3,2,1,0:T(8,128)} copy(f32[2,2,2,128,512]{4,3,2,1,0:T(8,128)} %shard_map.64) | data formatting | bytes 4194304

commit v3 on v2

--- a/solution.py
+++ b/solution.py
@@ -7,7 +7,7 @@
 from jax.sharding import PartitionSpec as P
 
 OFFMAX = 2
-UNROLL = 4
+UNROLL = 8
 MESH = pl.DeviceIdType.MESH
 F32 = jnp.float32
 BF16 = jnp.bfloat16
@@ -86,8 +86,8 @@
 def kernel(
     chunks, slabs, energies,
     lesser, retarded, coupling, numbers, shifts, beside_weight, out,
-    own, low, high, c_buf, w_buf, r_buf, left_buf, acc, half, near, far, comb,
-    local_sem, send_sem, recv_sem,
+    own, low, high, c_buf, w_buf, r_buf, left_buf, acc, half, near, far, comb, result,
+    store_sem, local_sem, send_sem, recv_sem,
 ):
     nf, size, _ = coupling.shape
     cut = size // chunks
@@ -137,7 +137,7 @@
         for k in range(chunks)
     ]
     load_r = pltpu.make_async_copy(retarded, r_buf, local_sem.at[1])
-    for load in [load_own, load_r] + load_c:
+    for load in [load_own] + load_c:
         load.start()
 
     for i in range(nf):
@@ -157,7 +157,6 @@
 
     pl.when(jnp.logical_not(has_low))(lambda: zero(low))
     pl.when(jnp.logical_not(has_high))(lambda: zero(high))
-    pl.when(jnp.logical_not(has_x))(lambda: zero(far))
 
     greeted = 4 + sum(condition.astype(jnp.int32) for condition in (has_low, has_high, has_x))
     pl.semaphore_wait(barrier, greeted)
@@ -189,6 +188,7 @@
         ups.append(go(remote(lesser.at[:, core, y, :, columns], low.at[k], above), has_high))
         downs.append(go(remote(lesser.at[:, core, y, :, columns], high.at[k], below), has_low))
 
+    load_r.start()
     load_own.wait()
     for load in load_c:
         load.wait()
@@ -216,7 +216,7 @@
             left_buf[e, :, columns] = left.astype(BF16)
             return carry
 
-        lax.fori_loop(0, number, body, 0, unroll=UNROLL)
+        lax.fori_loop(0, number, body, 0, unroll=min(UNROLL, number))
 
     def right_side(k, e):
         return by_rows(left_buf[e], c_buf[k])
@@ -246,56 +246,75 @@
         left_side(0, e, 2 * nf, lambda j: 2 * nf + j)
         acc[e] = right_side(0, e)
 
-    to_near, to_far = [], []
-
-    def finish_self(e):
-        half[e] = (acc[e] + right_side(chunks - 1, e)).astype(BF16)
-        to_far.append(go(remote(half.at[e], far.at[e], beside), has_x))
-        to_near.append(go(remote(half.at[e], near.at[e], partner)))
-
     for k in range(1, chunks - 1):
         arrive(k)
         for e in range(2):
             left_side(k, e, 4 * nf, lambda j: j)
             acc[e] += right_side(k, e)
 
-    comb_across = [remote(comb.at[e, 0], comb.at[e, 2], across) for e in range(2)]
-    comb_near = [remote(comb.at[e, 0], comb.at[e, 1], partner) for e in range(2)]
-    comb_far = [remote(comb.at[e, 2], comb.at[e, 3], partner) for e in range(2)]
-
-    def combine(e, with_far):
-        to_near[e].wait_recv()
-        around = near[e].astype(F32)
+    pairs = [(e, h) for e in range(2) for h in range(2)]
+    to_far = {p: remote(half.at[p], far.at[p], beside) for p in pairs}
+    to_near = {p: remote(half.at[p], near.at[p], partner) for p in pairs}
+    comb_across = {(e, h): remote(comb.at[e, 0, h], comb.at[e, 2, h], across) for e, h in pairs}
+    comb_near = {(e, h): remote(comb.at[e, 0, h], comb.at[e, 1, h], partner) for e, h in pairs}
+    comb_far = {(e, h): remote(comb.at[e, 2, h], comb.at[e, 3, h], partner) for e, h in pairs}
+    last = chunks - 1
+    middle_column = size // 2
+
+    def finish_self(e, h):
+        columns = slice(h * middle_column, (h + 1) * middle_column)
+        total = acc[e, :, columns] + by_rows(left_buf[e], c_buf[last, columns, :])
+        half[e, h] = total.astype(BF16)
+        go(to_far[e, h], has_x)
+        go(to_near[e, h])
+
+    def combine(e, h, with_far):
+        to_near[e, h].wait_recv()
+        around = near[e, h].astype(F32)
         if with_far:
-            to_far[e].wait_recv()
-            around = around + far[e].astype(F32)
-        comb[e, 0] = (half[e].astype(F32) + beside_weight[core] * around).astype(BF16)
-        comb_across[e].start()
-        comb_near[e].start()
+            to_far[e, h].wait_recv()
+            around = around + far[e, h].astype(F32)
+        comb[e, 0, h] = (half[e, h].astype(F32) + beside_weight[core] * around).astype(BF16)
+        comb_across[e, h].start()
+        comb_near[e, h].start()
 
     alone = jnp.logical_not(has_x)
-    last = chunks - 1
+
+    def combine_alone(e, h):
+        pl.when(alone)(lambda: combine(e, h, False))
+
     arrive(last)
     left_side(last, 0, 4 * nf, lambda j: j)
-    finish_self(0)
+    finish_self(0, 0)
+    finish_self(0, 1)
+    combine_alone(0, 0)
     left_side(last, 1, 4 * nf, lambda j: j)
-    pl.when(alone)(lambda: combine(0, False))
-    finish_self(1)
-    pl.when(alone)(lambda: combine(1, False))
-    pl.when(has_x)(lambda: combine(0, True))
-    pl.when(has_x)(lambda: combine(1, True))
+    combine_alone(0, 1)
+    finish_self(1, 0)
+    finish_self(1, 1)
+    combine_alone(1, 0)
+    combine_alone(1, 1)
+    for e, h in pairs:
+        pl.when(has_x)(lambda e=e, h=h: combine(e, h, True))
 
     load_r.wait()
     rows = size // 4
     mine = pl.ds(pl.multiple_of(q * rows, rows), rows)
 
     def pass_on(e):
-        comb_across[e].wait_recv()
-        comb_far[e].start()
+        for h in range(2):
+            comb_across[e, h].wait_recv()
+            comb_far[e, h].start()
 
     def take(e):
-        comb_near[e].wait_recv()
-        comb_far[e].wait_recv()
+        for h in range(2):
+            comb_near[e, h].wait_recv()
+            comb_far[e, h].wait_recv()
+
+    def whole_sum(e, slot):
+        return jnp.concatenate([comb[e, slot, 0], comb[e, slot, 1]], axis=1)
+
+    stores = []
 
     for group in range(2):
         same = alone if group == 0 else has_x
@@ -305,18 +324,24 @@
             pl.when(same)(lambda e=e: pass_on(e))
             pl.when(jnp.logical_not(same))(lambda e=e: take(e))
             edge = jnp.concatenate([r_buf[e, s, 0, mine, :], r_buf[e, s, 1, mine, :]], axis=0)
-            with_real = jnp.dot(edge, comb[e, 2 * y + other], preferred_element_type=F32)
-            with_imag = jnp.dot(edge, comb[e, 2 * (1 - y) + other], preferred_element_type=F32)
+            with_real = jnp.dot(edge, whole_sum(e, 2 * y + other), preferred_element_type=F32)
+            with_imag = jnp.dot(edge, whole_sum(e, 2 * (1 - y) + other), preferred_element_type=F32)
             middle = jnp.concatenate(
                 [with_real[:rows] - with_imag[rows:], with_imag[:rows] + with_real[rows:]], axis=0
             ).astype(BF16)
             by_real = by_rows(middle, r_buf[e, s, 0])
             by_imag = by_rows(middle, r_buf[e, s, 1])
-            out[e, s, 0] = by_real[:rows] + by_imag[rows:]
-            out[e, s, 1] = by_real[rows:] - by_imag[:rows]
-
-    for copy in comb_across + comb_near + comb_far:
-        copy.wait_send()
+            result[e, group, 0] = by_real[:rows] + by_imag[rows:]
+            result[e, group, 1] = by_real[rows:] - by_imag[:rows]
+            store = pltpu.make_async_copy(result.at[e, group], out.at[e, s], store_sem.at[e, group])
+            store.start()
+            stores.append(store)
+
+    for copies in (comb_across, comb_near, comb_far):
+        for p in pairs:
+            copies[p].wait_send()
+    for store in stores:
+        store.wait()
     for condition, copy in sent:
         under(condition, copy.wait_send)
 
@@ -325,13 +350,13 @@
     nf, size, _ = coupling.shape
     chunks = 2
     cut = size // chunks
-    copies = 3 + (nf + 6) * chunks + 10
+    copies = 3 + (nf + 6) * chunks + 20
     anywhere = pl.BlockSpec(memory_space=pl.ANY)
     return pl.pallas_call(
         functools.partial(kernel, chunks, lax.axis_size("slab"), lax.axis_size("energy")),
         out_shape=jax.ShapeDtypeStruct((2, 2, 2, size // 4, size), F32),
         in_specs=[anywhere] * 3 + [pl.BlockSpec(memory_space=pltpu.SMEM)] * 3,
-        out_specs=pl.BlockSpec(memory_space=pltpu.VMEM),
+        out_specs=anywhere,
         scratch_shapes=[
             pltpu.VMEM((2, size, size), BF16),
             pltpu.VMEM((chunks, 2, size, cut), BF16),
@@ -341,10 +366,12 @@
             pltpu.VMEM((2, 2, 2, size, size), BF16),
             pltpu.VMEM((2, size, 4 * nf * cut), BF16),
             pltpu.VMEM((2, size, size), F32),
-            pltpu.VMEM((2, size, size), BF16),
-            pltpu.VMEM((2, size, size), BF16),
-            pltpu.VMEM((2, size, size), BF16),
-            pltpu.VMEM((2, 4, size, size), BF16),
+            pltpu.VMEM((2, 2, size, size // 2), BF16),
+            pltpu.VMEM((2, 2, size, size // 2), BF16),
+            pltpu.VMEM((2, 2, size, size // 2), BF16),
+            pltpu.VMEM((2, 4, 2, size, size // 2), BF16),
+            pltpu.VMEM((2, 2, 2, size // 4, size), F32),
+            pltpu.SemaphoreType.DMA((2, 2)),
             pltpu.SemaphoreType.DMA((3 + nf * chunks,)),
             pltpu.SemaphoreType.DMA((copies,)),
             pltpu.SemaphoreType.DMA((copies,)),

time: 67.8 us -> 65.9 us (0.972)
  Pallas kernels: 64.6 us -> 62.6 us
    pallas_call x1, Pallas kernels: 64.6 us -> 62.6 us  [fast(): pl.pallas_call(functools.partial(kernel, chunks, lax.axis_size('slab'), l...]
where the time goes in v3:
time: 65.9 us; the launch traced here: 65.7 us
  Pallas kernels  62.6 us (95%)
  local copies, waits for them, and re-layouts  3.08 us (5%)
    pallas_call x1, Pallas kernels, fast(): pl.pallas_call(functools.partial(kernel, chunks, lax.axis_size('slab'), l...  62.6 us
    unnamed x1, local copies, waits for them, and re-layouts  3.08 us

profile of v3, /device:TPU:0, one launch (start us, length us, event | category | flops | bytes accessed | tf_op | source)
XLA Modules:
  0.0 65.7 jit_solution(12298599608324955963)
XLA Ops:
  0.0 62.6 %shard_map.64 = f32[2,2,2,128,512]{4,3,2,1,0:T(8,128)} custom-call(bf16[2,2,2,512,512]{4,3,2,1,0:T(8,128)(2,1)} %lesser.1, bf16[2,2,2,512,512]{4,3,2,1,0:T(8,128)(2,1)} %retarded.1, bf16[2,512,512]{2,1,0:T(8,128)(2,1)} %coupling.1, f32[2]{0:T(128)} %numbers.1, s32[2]{0:T(128)} %shifts.1, f32[2]{0:T(128)} %beside_weight.1), custom_call_target="tpu_custom_call" | custom-call | tf_op jit(solution)/shard_map/pallas_call | solution.py:355
  62.6 3.1 %copy.8 = f32[2,2,2,128,512]{4,3,2,1,0:T(8,128)} copy(f32[2,2,2,128,512]{4,3,2,1,0:T(8,128)} %shard_map.64) | data formatting | bytes 4194304

commit v4 on v3

--- a/solution.py
+++ b/solution.py
@@ -331,8 +331,8 @@
             ).astype(BF16)
             by_real = by_rows(middle, r_buf[e, s, 0])
             by_imag = by_rows(middle, r_buf[e, s, 1])
-            result[e, group, 0] = by_real[:rows] + by_imag[rows:]
-            result[e, group, 1] = by_real[rows:] - by_imag[:rows]
+            result[e, group, 0] = (by_real[:rows] + by_imag[rows:]).astype(BF16)
+            result[e, group, 1] = (by_real[rows:] - by_imag[:rows]).astype(BF16)
             store = pltpu.make_async_copy(result.at[e, group], out.at[e, s], store_sem.at[e, group])
             store.start()
             stores.append(store)
@@ -354,7 +354,7 @@
     anywhere = pl.BlockSpec(memory_space=pl.ANY)
     return pl.pallas_call(
         functools.partial(kernel, chunks, lax.axis_size("slab"), lax.axis_size("energy")),
-        out_shape=jax.ShapeDtypeStruct((2, 2, 2, size // 4, size), F32),
+        out_shape=jax.ShapeDtypeStruct((2, 2, 2, size // 4, size), BF16),
         in_specs=[anywhere] * 3 + [pl.BlockSpec(memory_space=pltpu.SMEM)] * 3,
         out_specs=anywhere,
         scratch_shapes=[
@@ -370,7 +370,7 @@
             pltpu.VMEM((2, 2, size, size // 2), BF16),
             pltpu.VMEM((2, 2, size, size // 2), BF16),
             pltpu.VMEM((2, 4, 2, size, size // 2), BF16),
-            pltpu.VMEM((2, 2, 2, size // 4, size), F32),
+            pltpu.VMEM((2, 2, 2, size // 4, size), BF16),
             pltpu.SemaphoreType.DMA((2, 2)),
             pltpu.SemaphoreType.DMA((3 + nf * chunks,)),
             pltpu.SemaphoreType.DMA((copies,)),
@@ -379,7 +379,7 @@
         compiler_params=pltpu.CompilerParams(
             collective_id=0, has_side_effects=True, vmem_limit_bytes=60 << 20
         ),
-    )(lesser, retarded, coupling, occupations, offsets, intersection)
+    )(lesser, retarded, coupling, occupations, offsets, intersection).astype(F32)
 
 
 def solution(mesh):

time: 65.9 us -> 65.5 us (level)
  local copies, waits for them, and re-layouts: 3.08 us -> 0 us
  other arithmetic: 0 us -> 2.83 us
    unnamed x1 -> x0, local copies, waits for them, and re-layouts: 3.08 us -> none
    convert_element_type x0 -> x1, other arithmetic: none -> 2.83 us  [fast(): return pl.pallas_call(functools.partial(kernel, chunks, lax.axis_size('sl...]
where the time goes in v4:
time: 65.5 us; the launch traced here: 65.3 us
  Pallas kernels  62.5 us (95%)
  other arithmetic  2.83 us (4%)
    pallas_call x1, Pallas kernels, fast(): pl.pallas_call(functools.partial(kernel, chunks, lax.axis_size('slab'), l...  62.5 us
    convert_element_type x1, other arithmetic, fast(): return pl.pallas_call(functools.partial(kernel, chunks, lax.axis_size('sl...  2.83 us

profile of v4, /device:TPU:0, one launch (start us, length us, event | category | flops | bytes accessed | tf_op | source)
XLA Modules:
  0.0 65.3 jit_solution(17065191589711349963)
XLA Ops:
  0.0 62.5 %shard_map.64 = bf16[2,2,2,128,512]{4,3,2,1,0:T(8,128)(2,1)} custom-call(bf16[2,2,2,512,512]{4,3,2,1,0:T(8,128)(2,1)} %lesser.1, bf16[2,2,2,512,512]{4,3,2,1,0:T(8,128)(2,1)} %retarded.1, bf16[2,512,512]{2,1,0:T(8,128)(2,1)} %coupling.1, f32[2]{0:T(128)} %numbers.1, s32[2]{0:T(128)} %shifts.1, f32[2]{0:T(128)} %beside_weight.1), custom_call_target="tpu_custom_call" | custom-call | tf_op jit(solution)/shard_map/pallas_call | solution.py:355
  62.5 2.8 %convert_element_type.3 = f32[2,2,2,128,512]{4,3,2,1,0:T(8,128)} convert(bf16[2,2,2,128,512]{4,3,2,1,0:T(8,128)(2,1)} %shard_map.64) | non-fusion elementwise | flops 524288 | bytes 3145728 | tf_op jit(solution)/shard_map/convert_element_type | solution.py:382
